TPU v7x, 32 devices: a whole 2x2x4 slice. The times are simulated.
32 devices in a mesh: grp: 4 (over y, x), dev: 8 (over z, core).
Axes of the slice: x: 2, y: 2, z: 4, core: 2. Of those that a mesh axis runs over, the one named last changes fastest.
Arguments:
- reach: bfloat16 [128, 64, 1326], P(('grp', 'dev')), may hold values from 0.00029945374 to 0.0029907227
- stake: float32 [128], replicated, may hold values from 1 to 10
- hand_rank: int32 [64, 1326], P(('grp', 'dev')), may hold values from 0 to 7461
- hand_live: int32 [64, 1326], P(('grp', 'dev')), may hold values 0 or 1
- board_seqs: int32 [64], P(('grp', 'dev')), may hold values from 1 to 128, 4096 in all
- board_turn: int32 [64, 1], replicated, may hold values from 0 to 15
- seq_parent: int32 [128], replicated, may hold values from 0 to 31, never falling along the last dimension, each value on 1 to 8 neighbouring positions
- set_parent: int32 [32], replicated, may hold values from 0 to 7, never falling along the last dimension, each value on 1 to 8 neighbouring positions
Outputs:
- river_values: float32 [32, 64, 1326], P(None, ('grp', 'dev'))
- turn_values: float32 [8, 16, 1326], replicated
Inputs may be any that keep to these rules, and one draw needn't show every extreme that they name: `seq_parent`: Non-decreasing; every value occurs, at most 8 times, exactly 8 times for some value. `set_parent`: Non-decreasing; every value occurs, at most 8 times, exactly 8 times for some value. `board_seqs`: some board has all 128 sequences live. `board_turn`: every turn board has at least one river board.
All inputs are finite; a program needn't handle non-finite values. No bound on the sum of `hand_live` or of `board_seqs` on one device may be relied on, other than what follows from the above.
Results may differ from a plain program's by a relative error of at most 0.0003.
Values may be sent and summed in bfloat16 or wider, within the bound.
A program may use at most 64 MiB of HBM per device.

v0:
```python
import jax
import jax.numpy as jnp
import numpy as np
from jax import lax
from jax.sharding import PartitionSpec as P

TURNS = 16
KIDS = 8


def hand_cards(count):
    card_pairs = [
        (lower_card, upper_card)
        for lower_card in range(52)
        for upper_card in range(lower_card + 1, 52)
    ]
    table = np.array(card_pairs[:count], dtype=np.int32)
    return (jnp.asarray(table[:, 0]), jnp.asarray(table[:, 1]))


def apart_table(count):
    first_card, second_card = hand_cards(count)
    return (
        (first_card[:, None] != first_card[None, :])
        & (first_card[:, None] != second_card[None, :])
        & (second_card[:, None] != first_card[None, :])
        & (second_card[:, None] != second_card[None, :])
    )


def payoff_matrix(ranks, live, apart):
    both_live = live[:, None] * live[None, :] > 0
    signs = jnp.sign(ranks[:, None] - ranks[None, :]).astype(jnp.bfloat16)
    return jnp.where(apart & both_live, signs, jnp.bfloat16(0.0))


def children(parent, count_sets, most):
    set_iota = jnp.arange(count_sets, dtype=jnp.int32)
    counts = jnp.sum((parent[None, :] == set_iota[:, None]).astype(jnp.int32), axis=1)
    starts = jnp.cumsum(counts) - counts
    kid_iota = jnp.arange(most, dtype=jnp.int32)
    index = jnp.minimum(starts[:, None] + kid_iota[None, :], parent.shape[0] - 1)
    valid = kid_iota[None, :] < counts[:, None]
    return (index, valid)


def segment_best(values, index, valid):
    picked = values[index]
    shape = valid.shape + (1,) * (values.ndim - 1)
    return jnp.max(jnp.where(valid.reshape(shape), picked, -jnp.inf), axis=1)


def local(reach, stake, hand_rank, hand_live, board_seqs, board_turn, seq_parent, set_parent):
    moved = lax.all_to_all(reach, ("grp", "dev"), split_axis=1, concat_axis=0, tiled=True)
    total_seqs = moved.shape[0]
    local_boards = moved.shape[1]
    hands = moved.shape[2]
    river_sets = set_parent.shape[0]
    apart = apart_table(hands)
    kid_index, kid_valid = children(seq_parent, river_sets, KIDS)
    seq_iota = jnp.arange(total_seqs, dtype=jnp.int32)
    river_list = []
    for board in range(local_boards):
        live_rows = (seq_iota < board_seqs[board]).astype(jnp.bfloat16)
        rows = moved[:, board, :] * live_rows[:, None]
        matrix = payoff_matrix(hand_rank[board], hand_live[board], apart)
        product = lax.dot_general(
            rows, matrix, (((1,), (1,)), ((), ())), preferred_element_type=jnp.float32
        )
        leaf = product * stake[:, None]
        river_list.append(segment_best(leaf, kid_index, kid_valid))
    river = jnp.stack(river_list, axis=1)
    turn_iota = jnp.arange(TURNS, dtype=jnp.int32)
    devices = lax.axis_size(("grp", "dev"))
    owned_sets = river_sets // devices
    owned = lax.all_to_all(river, ("grp", "dev"), split_axis=0, concat_axis=1, tiled=True)
    onehot = (board_turn[:, 0][None, :] == turn_iota[:, None]).astype(jnp.float32)
    chance = jnp.einsum("tb,pbh->pth", onehot, owned, precision=lax.Precision.HIGHEST)
    set_count = river_sets // 4
    set_iota = jnp.arange(set_count, dtype=jnp.int32)
    first_set = lax.axis_index(("grp", "dev")) * owned_sets
    parent_set = set_parent[first_set + 0]
    chosen = (set_iota == parent_set)[:, None, None]
    candidate = jnp.where(chosen, chance[0][None], -jnp.inf)
    best = lax.pmax(candidate, ("grp", "dev"))
    return (river, best)


def solution(mesh):
    in_specs = (
        P(("grp", "dev"), None, None),
        P(),
        P(("grp", "dev"), None),
        P(("grp", "dev"), None),
        P(("grp", "dev")),
        P(),
        P(),
        P(),
    )
    out_specs = (P(None, ("grp", "dev"), None), P())
    return jax.shard_map(local, mesh=mesh, in_specs=in_specs, out_specs=out_specs, check_vma=False)
```

profile of v0, /device:TPU:1, one launch (start us, length us, event | category | flops | bytes accessed | tf_op | source)
XLA Modules:
  0.0 209.7 jit_solution(5315465424213060597)
XLA Ops:
  7.2 0.0 copy-start.4
  7.2 0.0 copy-start.2
  7.2 0.0 copy-start
  7.2 0.0 copy-start.1
  7.2 2.5 %copy.39 = bf16[4,64,1326]{2,0,1:T(4,128)(2,1)} copy(bf16[4,64,1326]{2,1,0:T(8,128)(2,1)} %param.10) | data formatting | bytes 1357824 | tf_op args[0]
  9.8 7.1 %all-to-all-start = ((bf16[4,64,1326]{2,0,1:T(4,128)(2,1)}), bf16[4,64,1326]{2,0,1:T(4,128)(2,1)S(1)}, u32[]{:S(2)}, u32[]{:S(2)}) async-start(bf16[4,64,1326]{2,0,1:T(4,128)(2,1)} %copy.39), calls=%async_computation | async-start | bytes 1441792 | tf_op jit(solution)/shard_map/all_to_all | solution.py:54
  16.9 0.0 copy-done.4
  16.9 0.1 convert_reduce_fusion
  17.0 0.1 copy.42
  17.1 0.1 reduce-window.8
  17.1 0.1 reduce.2
  17.3 0.1 compare_select_fusion
  17.3 0.1 reshape.133
  17.4 0.6 fusion.26
  18.0 0.6 compare_convert_fusion
  18.7 0.7 compare_convert_fusion.1
  19.4 0.1 slice_reduce_fusion.2
  19.5 0.1 iota_compare_fusion.1
  19.6 17.3 %all-to-all-done = bf16[4,64,1326]{2,0,1:T(4,128)(2,1)S(1)} async-done(((bf16[4,64,1326]{2,0,1:T(4,128)(2,1)}), bf16[4,64,1326]{2,0,1:T(4,128)(2,1)S(1)}, u32[]{:S(2)}, u32[]{:S(2)}) %all-to-all-start) | async-done | bytes 678944 | tf_op jit(solution)/shard_map/all_to_all | solution.py:54
  36.8 0.6 copy.40
  37.4 0.0 copy-start.5
  37.4 0.0 copy-start.7
  37.4 0.0 copy-start.8
  37.4 1.0 fusion.25
  38.4 1.0 copy.44
  39.5 4.6 %fusion.11 = f32[128,1326]{0,1:T(8,128)S(1)} fusion(s32[1326]{0:T(1024)S(1)} %get-tuple-element.13, s32[1326]{0:T(1024)S(1)} %get-tuple-element.20, s32[1326]{0:T(1024)S(1)} %copy-done.8, s32[1326]{0:T(1024)S(1)} %copy-done.7, bf16[128,1,1326]{0,2,1:T(8,128)(2,1)S(1)} %copy.44, f32[128]{0:T(128)S(1)} %copy-done.5, bf16[128]{0:T(256)(128)(2,1)S(1)} %compare_convert_fusion), kind=kOutput, calls=%fused_computation.14 | convolution fusion | flops 475073984 | bytes 1040352 | tf_op jit(solution)/shard_map/dot_general | solution.py:67
  44.1 0.3 copy.45
  44.4 1.2 copy.41
  45.5 4.6 %fusion.8 = f32[128,1326]{0,1:T(8,128)S(1)} fusion(s32[1326]{0:T(1024)S(1)} %get-tuple-element.12, s32[1326]{0:T(1024)S(1)} %get-tuple-element.21, s32[1326]{0:T(1024)S(1)} %copy-done.8, s32[1326]{0:T(1024)S(1)} %copy-done.7, bf16[128,1,1326]{0,2,1:T(8,128)(2,1)S(1)} %copy.41, f32[128]{0:T(128)S(1)} %copy-done.5, bf16[128]{0:T(256)(128)(2,1)S(1)} %compare_convert_fusion.1), kind=kOutput, calls=%fused_computation.13 | convolution fusion | flops 475073984 | bytes 1040352 | tf_op jit(solution)/shard_map/dot_general | solution.py:67
  50.2 0.3 copy.43
  50.4 1.2 gather_fusion.1
  51.7 2.3 %gather_fusion = f32[256,1326]{1,0:T(8,128)} fusion(f32[128,1326]{1,0:T(8,128)S(1)} %copy.43, s32[1024]{0:T(1024)S(1)} %pad_clamp_fusion), kind=kCustom, calls=%fused_computation | custom fusion | bytes 2716672 | tf_op jit(solution)/shard_map/gather | solution.py:48
  54.0 2.3 %fusion.17 = (f32[32,1326]{1,0:T(8,128)S(1)}, f32[32,1326]{1,0:T(8,128)S(1)}) fusion(f32[256,1326]{1,0:T(8,128)} %gather_fusion, pred[32,8]{1,0:T(8,128)(4,1)S(1)} %iota_compare_fusion.1, f32[256,1326]{1,0:T(8,128)S(1)} %gather_fusion.1), kind=kLoop, calls=%fused_computation.21 | loop fusion | flops 1272960 | bytes 3055360 | tf_op jit(solution)/shard_map/reduce_max | solution.py:50
  56.3 0.0 copy-start.6
  56.3 0.0 copy-start.3
  56.4 1.0 copy.47
  57.4 3.0 %all-to-all-start.1 = ((f32[32,2,1326]{2,1,0:T(2,128)}), f32[32,2,1326]{2,1,0:T(2,128)S(1)}, u32[]{:S(2)}, u32[]{:S(2)}) async-start(f32[32,2,1326]{2,1,0:T(2,128)} %copy.47), calls=%async_computation.1 | async-start | bytes 720896 | tf_op jit(solution)/shard_map/all_to_all | solution.py:76
  60.4 0.0 all-reduce.2.cloned.1.call-start
  60.5 0.6 dynamic_slice.3
  61.1 0.6 iota_compare_fusion.4
  61.7 11.5 %all-to-all-done.1 = f32[32,2,1326]{2,1,0:T(2,128)S(1)} async-done(((f32[32,2,1326]{2,1,0:T(2,128)}), f32[32,2,1326]{2,1,0:T(2,128)S(1)}, u32[]{:S(2)}, u32[]{:S(2)}) %all-to-all-start.1) | async-done | bytes 339488 | tf_op jit(solution)/shard_map/all_to_all | solution.py:76
  73.3 0.2 reshape.130
  73.5 0.0 copy-done.3
  73.5 0.2 convolution_bitcast_fusion
  73.8 1.0 broadcast_select_fusion
  74.7 0.0 all-reduce.2.cloned.1.call-update
  74.8 126.0 %all-reduce.2.cloned.1.call-done = f32[8,16,1326]{2,1,0:T(8,128)} async-done(((f32[8,16,1326]{2,1,0:T(8,128)}), f32[8,16,1326]{2,1,0:T(8,128)}) %all-reduce.2.cloned.1.call-update) | async-done | bytes 678928 | tf_op jit(solution)/shard_map/pmax | solution.py:85
  200.8 2.0 copy.49
  (10 shorter events, 0.1 us)
Async XLA Ops:
  7.2 9.7 %copy-start.4 = (s32[128]{0:T(128)S(1)}, s32[128]{0:T(128)}, u32[]{:S(2)}) copy-start(s32[128]{0:T(128)} %param.16) | copy-start | bytes 1540
  7.2 10.3 %copy-start.2 = (s32[2]{0:T(128)S(1)}, s32[2]{0:T(128)}, u32[]{:S(2)}) copy-start(s32[2]{0:T(128)} %param.14) | copy-start | bytes 28
  7.2 12.2 %copy-start = (s32[2,1326]{1,0:T(2,128)S(1)}, s32[2,1326]{1,0:T(2,128)}, u32[]{:S(2)}) copy-start(s32[2,1326]{1,0:T(2,128)} %param.12) | copy-start | bytes 31828
  7.2 12.2 %copy-start.1 = (s32[2,1326]{1,0:T(2,128)S(1)}, s32[2,1326]{1,0:T(2,128)}, u32[]{:S(2)}) copy-start(s32[2,1326]{1,0:T(2,128)} %param.13) | copy-start | bytes 31828
  9.8 27.1 %all-to-all-start = ((bf16[4,64,1326]{2,0,1:T(4,128)(2,1)}), bf16[4,64,1326]{2,0,1:T(4,128)(2,1)S(1)}, u32[]{:S(2)}, u32[]{:S(2)}) async-start(bf16[4,64,1326]{2,0,1:T(4,128)(2,1)} %copy.39), calls=%async_computation | async-start | bytes 1441792 | tf_op jit(solution)/shard_map/all_to_all | solution.py:54
  37.4 2.0 copy-start.5
  37.4 2.0 copy-start.7
  37.4 2.0 copy-start.8
  56.3 4.2 %copy-start.6 = (s32[32]{0:T(128)S(1)}, s32[32]{0:T(128)}, u32[]{:S(2)}) copy-start(s32[32]{0:T(128)} %param.17) | copy-start | bytes 388
  56.3 17.2 %copy-start.3 = (s32[64,1]{0,1:T(1,128)S(1)}, s32[64,1]{0,1:T(1,128)}, u32[]{:S(2)}) copy-start(s32[64,1]{0,1:T(1,128)} %param.15) | copy-start | bytes 772
  57.4 15.9 %all-to-all-start.1 = ((f32[32,2,1326]{2,1,0:T(2,128)}), f32[32,2,1326]{2,1,0:T(2,128)S(1)}, u32[]{:S(2)}, u32[]{:S(2)}) async-start(f32[32,2,1326]{2,1,0:T(2,128)} %copy.47), calls=%async_computation.1 | async-start | bytes 720896 | tf_op jit(solution)/shard_map/all_to_all | solution.py:76
  60.4 140.4 %all-reduce.2.cloned.1.call-start = ((), (), s32[]{:S(2)}) async-start(), calls=%async_computation.2 | async-start | bytes 1441792 | tf_op jit(solution)/shard_map/pmax | solution.py:85
Sparse Core Ops, SparseCore 0:
  74.9 125.8 all-reduce.1
where the time goes:
time: 210 us
  waiting for transfers between devices  155 us (74%)
  local copies, waits for them, and re-layouts  15.1 us (7%)
  between operations  14.3 us (7%)
  starting transfers between devices  10.2 us (5%)
  matrix products  9.5 us (5%)
  other arithmetic  5.76 us (3%)
    pmax x1, waiting for transfers between devices, local(): best = lax.pmax(candidate, ('grp', 'dev'))  126 us
    all_to_all x1, waiting for transfers between devices, local(): lax.all_to_all(reach, ('grp', 'dev'), split_axis=1, concat_axis=0, tiled=...  17.3 us
    all_to_all x1, waiting for transfers between devices, local(): lax.all_to_all(river, ('grp', 'dev'), split_axis=0, concat_axis=1, tiled=...  11.5 us
    dot_general x2, matrix products, local(): lax.dot_general(rows, matrix, (((1,), (1,)), ((), ())), preferred_element...  9.25 us
    all_to_all x1, starting transfers between devices, local(): lax.all_to_all(reach, ('grp', 'dev'), split_axis=1, concat_axis=0, tiled=...  7.1 us
    unnamed x21, local copies, waits for them, and re-layouts  5.63 us
  transfers between devices with their start and end apart: 3, of which 3 were waited for; matrix products, arithmetic and copies ran while one was open for 2% of the time, Pallas kernels for 0%

commit v1 on v0

v1 whole, which is shorter than its diff:
```python
import functools

import jax
import jax.numpy as jnp
import numpy as np
from jax import lax
from jax.experimental import pallas as pl
from jax.experimental.pallas import tpu as pltpu
from jax.sharding import PartitionSpec as P

TURNS = 16
KIDS = 8
LANE = 128
MESH = pl.DeviceIdType.MESH


def card_bits(count, padded):
    pairs = [(a, b) for a in range(52) for b in range(a + 1, 52)][:count]
    words = np.zeros((2, padded), np.int32)
    for hand, pair in enumerate(pairs):
        for card in pair:
            words[card // 26, hand] |= 1 << (card % 26)
    return words


def children(parent, count_sets, most):
    set_iota = jnp.arange(count_sets, dtype=jnp.int32)
    starts = jnp.sum((parent[None, :] < set_iota[:, None]).astype(jnp.int32), axis=1)
    ends = jnp.sum((parent[None, :] <= set_iota[:, None]).astype(jnp.int32), axis=1)
    kid_iota = jnp.arange(most, dtype=jnp.int32)
    return jnp.minimum(starts[:, None] + kid_iota[None, :], ends[:, None] - 1)


def kernel(G, D, hands, kids_ref, turn_ref, parent_col, reach_ref, rank_ref, live_ref, bits_ref, scale_ref,
           river_out, turn_out,
           moved, rows_f, rows_i, cols_f, cols_i, pay, leaf, river, gathered, chance, best,
           send_a, recv_a, send_c, recv_c, send_e, recv_e, own_sem):
    n = G * D
    tiles = -(-hands // LANE)
    width = tiles * LANE
    sets = river_out.shape[0]
    turn_sets = turn_out.shape[0]
    g, d = lax.axis_index("grp"), lax.axis_index("dev")
    core = lax.rem(d, 2)
    me = g * D + d

    def where_is(flat):
        return (flat // D, lax.rem(flat, D))

    barrier = pltpu.get_barrier_semaphore()

    @pl.loop(1, n)
    def _(k):
        pl.semaphore_signal(barrier, inc=1, device_id=where_is(lax.rem(me + k, n)), device_id_type=MESH)

    pl.semaphore_wait(barrier, n - 1)

    def send_reach(k):
        to = lax.rem(me + k, n)
        return pltpu.make_async_remote_copy(
            src_ref=reach_ref.at[to], dst_ref=moved.at[me], send_sem=send_a.at[k], recv_sem=recv_a.at[me],
            device_id=where_is(to), device_id_type=MESH)

    def got_reach(k):
        frm = lax.rem(me + k, n)
        return pltpu.make_async_remote_copy(
            src_ref=reach_ref.at[frm], dst_ref=moved.at[frm], send_sem=send_a.at[k], recv_sem=recv_a.at[frm],
            device_id=where_is(frm), device_id_type=MESH)

    own = pltpu.make_async_copy(reach_ref.at[me], moved.at[me], own_sem.at[0])
    own.start()

    @pl.loop(1, n)
    def _(k):
        send_reach(k).start()

    rows_f[...] = jnp.zeros_like(rows_f)
    rows_i[...] = jnp.zeros_like(rows_i)
    rows_f[0:2, 0:hands] = rank_ref[...].astype(jnp.float32)
    rows_i[0:2, 0:hands] = live_ref[...]
    dead = 1 - rows_i[0:2, :]
    low, high = bits_ref[0:1, :], bits_ref[1:2, :]
    ours = low + (1 << 26) + dead * (1 << 27)
    theirs = low + (1 << 27) + dead * (1 << 26)
    rows_i[0:2, :] = ours
    rows_i[2:3, :] = high
    rows_i[3:5, :] = theirs
    for tile in range(tiles):
        cut = slice(tile * LANE, (tile + 1) * LANE)
        cols_f[cut, :] = jnp.transpose(rows_f[:, cut])
        cols_i[cut, :] = jnp.transpose(rows_i[:, cut])

    @pl.loop(0, width // 16)
    def _(step):
        at = pl.ds(pl.multiple_of(step * 16, 16), 16)
        ranks, words = cols_f[at, :], cols_i[at, :]
        for board in range(2):
            shared = (rows_i[board:board + 1, :] & words[:, 3 + board:4 + board]) | (rows_i[2:3, :] & words[:, 2:3])
            sign = jnp.clip(rows_f[board:board + 1, :] - ranks[:, board:board + 1], -1.0, 1.0)
            pay[board, at, :] = jnp.where(shared == 0, sign, 0.0).astype(jnp.bfloat16)

    own.wait()

    @pl.loop(1, n)
    def _(k):
        got_reach(k).wait_recv()

    chunk = 32
    first = lax.broadcasted_iota(jnp.int32, (chunk * 8, 1), 0) % 8 < 4

    @pl.loop(0, n // chunk)
    def _(part):
        src = pl.ds(part * chunk, chunk)
        rows = moved[src].astype(jnp.float32).reshape(chunk * 8, width).astype(jnp.bfloat16)
        at = pl.ds(pl.multiple_of(part * chunk * 8, chunk * 8), chunk * 8)
        scale = scale_ref[at, :]
        for nt in range(leaf.shape[1] // 256):
            cut = slice(nt * 256, (nt + 1) * 256)
            one = jnp.dot(rows, pay[0, :, cut], preferred_element_type=jnp.float32)
            two = jnp.dot(rows, pay[1, :, cut], preferred_element_type=jnp.float32)
            leaf[at, cut] = jnp.where(first, one, two) * scale

    @pl.loop(0, sets)
    def _(p):
        for board in range(2):
            row = leaf[pl.ds(kids_ref[p * KIDS] + 4 * board, 1), 0:width]
            for kid in range(1, KIDS):
                row = jnp.maximum(row, leaf[pl.ds(kids_ref[p * KIDS + kid] + 4 * board, 1), 0:width])
            river[board, pl.ds(p, 1), :] = row
            river_out[p, board:board + 1, :] = row[:, 0:hands]

    zs = (1, 2, 0) + tuple(range(3, D // 2))
    owner_g = [j % G for j in range(tiles)]
    owner_d = [(2 * zs[(j // G) % len(zs)] + (j % G + j // G) % 2) % D for j in range(tiles)]

    def send_river(j):
        return pltpu.make_async_remote_copy(
            src_ref=river.at[:, :, pl.ds(j * LANE, LANE)], dst_ref=gathered.at[pl.ds(2 * me, 2)],
            send_sem=send_c.at[j], recv_sem=recv_c.at[me], device_id=(owner_g[j], owner_d[j]), device_id_type=MESH)

    def is_owner(j):
        return (g == owner_g[j]) & (d == owner_d[j])

    def own_river(j):
        return pltpu.make_async_copy(
            river.at[:, :, pl.ds(j * LANE, LANE)], gathered.at[pl.ds(2 * me, 2)], own_sem.at[1])

    for j in range(tiles):
        @pl.when(is_owner(j))
        def _():
            own_river(j).start()

        @pl.when(jnp.logical_not(is_owner(j)))
        def _():
            send_river(j).start()

    def send_turn(j, slot, to):
        piece = best.at[:, :, pl.ds(j * LANE, LANE)]
        return pltpu.make_async_remote_copy(
            src_ref=piece, dst_ref=piece, send_sem=send_e.at[j, slot], recv_sem=recv_e.at[j],
            device_id=to, device_id_type=MESH)

    def got_turn(j):
        return send_turn(j, 0, (g, d))

    lines = D // 2
    any_owner = functools.reduce(jnp.logical_or, [is_owner(j) for j in range(tiles)])

    @pl.when(any_owner)
    def _():
        pltpu.make_async_copy(river.at[:, :, pl.ds(0, LANE)], gathered.at[pl.ds(2 * me, 2)], own_sem.at[1]).wait()

        @pl.loop(1, n)
        def _(k):
            frm = lax.rem(me + k, n)
            pltpu.make_async_remote_copy(
                src_ref=river.at[:, :, pl.ds(0, LANE)], dst_ref=gathered.at[pl.ds(2 * frm, 2)],
                send_sem=send_c.at[0], recv_sem=recv_c.at[frm], device_id=where_is(frm),
                device_id_type=MESH).wait_recv()

        group = 4
        psub = 32
        for turn0 in range(0, TURNS, group):
            for p0 in range(0, sets, psub):
                def add(b, accs):
                    block = gathered[b, p0:p0 + psub, :]
                    return tuple(
                        acc + jnp.where(turn_ref[b] == turn0 + i, 1.0, 0.0) * block for i, acc in enumerate(accs))
                accs = lax.fori_loop(
                    0, 2 * n, add, tuple(jnp.zeros((psub, LANE), jnp.float32) for _ in range(group)), unroll=8)
                for i in range(group):
                    chance[turn0 + i, p0:p0 + psub, :] = accs[i]

        parents = parent_col[...]

        @pl.loop(0, turn_sets)
        def _(q):
            chosen = parents == q
            rows = [jnp.max(jnp.where(chosen, chance[t], -jnp.inf), axis=0, keepdims=True) for t in range(TURNS)]
            value = jnp.concatenate(rows, axis=0)
            for j in range(tiles):
                @pl.when(is_owner(j))
                def _():
                    best[q, :, pl.ds(j * LANE, LANE)] = value

    def peers(j):
        return [(k, (g, 2 * lax.rem(d // 2 + k, lines) + core)) for k in range(1, lines)]

    def across(j):
        return [(lines - 1 + k, (lax.rem(g + k, G), d)) for k in range(1, G)]

    def pair(j):
        return [(lines - 1 + G, (g, d + 1 - 2 * core))]

    in_line = [(g == owner_g[j]) & (core == owner_d[j] % 2) for j in range(tiles)]
    has_core = [core == owner_d[j] % 2 for j in range(tiles)]
    for j in range(tiles):
        @pl.when(is_owner(j))
        def _():
            for slot, to in peers(j) + across(j) + pair(j):
                send_turn(j, slot, to).start()
    for j in range(tiles):
        @pl.when(in_line[j] & jnp.logical_not(is_owner(j)))
        def _():
            got_turn(j).wait_recv()
            for slot, to in across(j) + pair(j):
                send_turn(j, slot, to).start()
    for j in range(tiles):
        @pl.when(has_core[j] & jnp.logical_not(in_line[j]))
        def _():
            got_turn(j).wait_recv()
            for slot, to in pair(j):
                send_turn(j, slot, to).start()
    for j in range(tiles):
        @pl.when(jnp.logical_not(has_core[j]))
        def _():
            got_turn(j).wait_recv()

    turn_out[...] = best[:, :, 0:hands]

    for j in range(tiles):
        @pl.when(is_owner(j))
        def _():
            for slot, to in peers(j):
                send_turn(j, slot, to).wait_send()

        @pl.when(in_line[j])
        def _():
            for slot, to in across(j):
                send_turn(j, slot, to).wait_send()

        @pl.when(has_core[j])
        def _():
            for slot, to in pair(j):
                send_turn(j, slot, to).wait_send()

        @pl.when(jnp.logical_not(is_owner(j)))
        def _():
            send_river(j).wait_send()

    @pl.loop(1, n)
    def _(k):
        send_reach(k).wait_send()


def local(G, D, reach, stake, hand_rank, hand_live, board_seqs, board_turn, seq_parent, set_parent):
    n = G * D
    own_seqs, boards, hands = reach.shape
    seqs = stake.shape[0]
    sets = set_parent.shape[0]
    tiles = -(-hands // LANE)
    width = tiles * LANE
    wide = -(-width // 256) * 256
    staged = jnp.transpose(reach.reshape(own_seqs, n, 2, hands), (1, 2, 0, 3)).reshape(n, 2 * own_seqs, hands)
    staged = jnp.pad(staged, ((0, 0), (0, 0), (0, width - hands)))
    index = children(seq_parent, sets, KIDS)
    kids = ((index // 4) * 8 + index % 4).reshape(-1)
    live = jnp.arange(seqs, dtype=jnp.int32)[None, :] < board_seqs[:, None]
    scale = jnp.where(live, stake[None, :], 0.0).reshape(2, n, own_seqs)
    scale = jnp.transpose(scale, (1, 0, 2)).reshape(n * 8, 1)
    turn_sets = sets // 4
    vmem = pl.BlockSpec(memory_space=pltpu.VMEM)
    smem = pl.BlockSpec(memory_space=pltpu.SMEM)
    river, best = pl.pallas_call(
        functools.partial(kernel, G, D, hands),
        out_shape=(
            jax.ShapeDtypeStruct((sets, 2, hands), jnp.float32),
            jax.ShapeDtypeStruct((turn_sets, TURNS, hands), jnp.float32),
        ),
        in_specs=[smem, smem, vmem, vmem, vmem, vmem, vmem, vmem],
        out_specs=(vmem, vmem),
        scratch_shapes=[
            pltpu.VMEM((n, 8, width), jnp.bfloat16),
            pltpu.VMEM((8, wide), jnp.float32),
            pltpu.VMEM((8, wide), jnp.int32),
            pltpu.VMEM((width, 8), jnp.float32),
            pltpu.VMEM((width, 8), jnp.int32),
            pltpu.VMEM((2, width, wide), jnp.bfloat16),
            pltpu.VMEM((n * 8, wide), jnp.float32),
            pltpu.VMEM((2, sets, width), jnp.float32),
            pltpu.VMEM((2 * n, sets, LANE), jnp.float32),
            pltpu.VMEM((TURNS, sets, LANE), jnp.float32),
            pltpu.VMEM((turn_sets, TURNS, width), jnp.float32),
            pltpu.SemaphoreType.DMA((n,)),
            pltpu.SemaphoreType.DMA((n,)),
            pltpu.SemaphoreType.DMA((tiles,)),
            pltpu.SemaphoreType.DMA((n,)),
            pltpu.SemaphoreType.DMA((tiles, D // 2 + G)),
            pltpu.SemaphoreType.DMA((tiles,)),
            pltpu.SemaphoreType.DMA((2,)),
        ],
        compiler_params=pltpu.CompilerParams(
            collective_id=0, has_side_effects=True, vmem_limit_bytes=56 << 20),
    )(kids, board_turn[:, 0], set_parent[:, None], staged, hand_rank, hand_live,
      jnp.asarray(card_bits(hands, wide)), scale)
    return river, best


def solution(mesh):
    axes = ("grp", "dev")
    in_specs = (
        P(axes, None, None),
        P(),
        P(axes, None),
        P(axes, None),
        P(axes),
        P(),
        P(),
        P(),
    )
    out_specs = (P(None, axes, None), P())
    body = functools.partial(local, mesh.shape["grp"], mesh.shape["dev"])
    return jax.shard_map(body, mesh=mesh, in_specs=in_specs, out_specs=out_specs, check_vma=False)
```

time: 210 us -> 67.4 us (0.32)
  the two profiles are of different devices: /device:TPU:1 before, /device:TPU:27 now
where the time goes in v1:
time: 67.4 us; the launch traced here: 67.2 us
  Pallas kernels  56.5 us (84%)
  local copies, waits for them, and re-layouts  9.19 us (14%)
  other arithmetic  0.87 us (1%)
  between operations  0.69 us (1%)
    pallas_call x1, Pallas kernels, local(): pl.pallas_call(functools.partial(kernel, G, D, hands), out_shape=(jax.Sha...  56.5 us
    unnamed x12, local copies, waits for them, and re-layouts  4.6 us
    reshape x1, local copies, waits for them, and re-layouts, local(): reach.reshape(own_seqs, n, 2, hands)  1.67 us

profile of v1, /device:TPU:27, one launch (start us, length us, event | category | flops | bytes accessed | tf_op | source)
XLA Modules:
  0.0 67.2 jit_solution(16610364966636044616)
XLA Ops:
  0.6 0.0 copy-start.4
  0.6 0.6 copy-done.4
  1.3 0.1 convert_reduce_fusion.1
  1.4 0.1 add_minimum_fusion
  1.5 0.1 min.14
  1.6 0.0 copy-start.2
  1.6 0.6 fusion.kids_ref
  2.2 0.1 copy-done.2
  2.2 0.0 copy-start.3
  2.2 0.1 broadcast_in_dim.13
  2.3 0.6 copy-done.3
  2.9 0.7 %copy.17.parent_col = s32[32,1]{1,0:T(8,128)} copy(s32[32,1]{0,1:T(1,128)S(1)} %bitcast.7) | data formatting | bytes 256 | tf_op jit(solution)/shard_map/broadcast_in_dim | solution.py:314
  3.6 0.0 copy-start.1
  3.6 0.6 copy-done.1
  4.2 0.1 compare_select_fusion
  4.3 0.8 %select_n.32.scale_ref = f32[256,1]{1,0:T(8,128)} reshape(f32[32,2,4]{2,1,0:T(2,128)S(1)} %compare_select_fusion) | data formatting | bytes 2048 | tf_op jit(solution)/shard_map/jit(_where)/select_n | solution.py:279
  5.1 1.7 %copy.19 = bf16[4,64,1326]{2,0,1:T(4,128)(2,1)S(1)} copy(bf16[4,64,1326]{2,1,0:T(8,128)(2,1)} %param.9) | data formatting | bytes 1357824 | tf_op jit(solution)/shard_map/reshape | solution.py:274
  6.8 0.3 reshape.74
  7.1 0.9 %pad.4.reach_ref = bf16[32,8,1408]{2,1,0:T(8,128)(2,1)} pad(bf16[32,8,1326]{2,1,0:T(8,128)(2,1)S(1)} %reshape.74, bf16[]{:T(256)} %constant.38.clone.1), padding=0_0x0_0x0_82 | pad | bytes 1399810 | tf_op jit(solution)/shard_map/jit(_pad)/pad | solution.py:275
  8.0 56.5 %shard_map.104 = (f32[32,2,1326]{2,1,0:T(2,128)}, f32[8,16,1326]{2,1,0:T(8,128)}) custom-call(s32[256]{0:T(256)} %fusion.kids_ref, s32[64]{0:T(128)} %bitcast.6, s32[32,1]{1,0:T(8,128)} %copy.17.parent_col, bf16[32,8,1408]{2,1,0:T(8,128)(2,1)} %pad.4.reach_ref, s32[2,1326]{1,0:T(2,128)} %rank_ref.1, s32[2,1326]{1,0:T(2,128)} %live_ref.1, ...), custom_call_target="tpu_custom_call" | custom-call | tf_op jit(solution)/shard_map/pallas_call | solution.py:284
  64.5 0.0 copy-start
  64.5 1.8 %copy.22 = f32[32,2,1326]{2,1,0:T(2,128)} copy(f32[32,2,1326]{2,1,0:T(2,128)} %get-tuple-element.6) | data formatting | bytes 678912
  66.3 0.0 copy-done
  66.3 0.9 %copy.23 = f32[8,16,1326]{2,1,0:T(8,128)} copy(f32[8,16,1326]{2,1,0:T(8,128)S(1)} %copy-done) | data formatting | bytes 1357824
  (2 shorter events, 0.0 us)
Async XLA Ops:
  0.6 0.7 copy-start.4
  1.6 0.7 copy-start.2
  2.2 0.7 copy-start.3
  3.6 0.7 copy-start.1
  64.5 1.8 %copy-start = (f32[8,16,1326]{2,1,0:T(8,128)S(1)}, f32[8,16,1326]{2,1,0:T(8,128)}, u32[]{:S(2)}) copy-start(f32[8,16,1326]{2,1,0:T(8,128)} %get-tuple-element.7) | copy-start | bytes 2036740

commit v2 on v1

v2 whole, which is shorter than its diff:
```python
import functools

import jax
import jax.numpy as jnp
import numpy as np
from jax import lax
from jax.experimental import pallas as pl
from jax.experimental.pallas import tpu as pltpu
from jax.sharding import PartitionSpec as P

TURNS = 16
KIDS = 8
LANE = 128
MESH = pl.DeviceIdType.MESH


def card_bits(count, padded):
    pairs = [(a, b) for a in range(52) for b in range(a + 1, 52)][:count]
    words = np.zeros((2, padded), np.int32)
    for hand, pair in enumerate(pairs):
        for card in pair:
            words[card // 26, hand] |= 1 << (card % 26)
    return words


def kernel(G, D, hands, turn_ref, board_seqs_ref, seq_parent_ref, set_parent_ref, stake_ref, reach_ref, rank_ref,
           live_ref, bits_ref,
           river_out, turn_out,
           kids_ref, scale_ref, parent_col, turn_rows, moved, dense, rows_f, rows_i, cols_f, cols_i, pay, leaf, river,
           packed, gathered, chance, best,
           send_a, recv_a, send_c, recv_c, send_e, recv_e, own_sem):
    n = G * D
    tiles = -(-hands // LANE)
    width = tiles * LANE
    sets = river_out.shape[0]
    turn_sets = turn_out.shape[0]
    g, d = lax.axis_index("grp"), lax.axis_index("dev")
    core = lax.rem(d, 2)
    me = g * D + d

    def where_is(flat):
        return (flat // D, lax.rem(flat, D))

    barrier = pltpu.get_barrier_semaphore()

    @pl.loop(1, n)
    def _(k):
        pl.semaphore_signal(barrier, inc=1, device_id=where_is(lax.rem(me + k, n)), device_id_type=MESH)

    pl.semaphore_wait(barrier, n - 1)

    bits = n.bit_length() - 1
    order = [2, 1] + [i for i in range(3, bits)] + [0]

    def partner(k):
        to = me
        for place, bit in enumerate(order):
            flip = lax.rem(k // (1 << place), 2)
            have = lax.rem(me // (1 << bit), 2)
            to = to + (flip - 2 * flip * have) * (1 << bit)
        return to

    def send_reach(k):
        to = partner(k)
        return pltpu.make_async_remote_copy(
            src_ref=reach_ref.at[to], dst_ref=moved.at[me], send_sem=send_a.at[k], recv_sem=recv_a.at[me],
            device_id=where_is(to), device_id_type=MESH)

    def got_reach(k):
        frm = lax.rem(me + k, n)
        return pltpu.make_async_remote_copy(
            src_ref=reach_ref.at[frm], dst_ref=moved.at[frm], send_sem=send_a.at[k], recv_sem=recv_a.at[frm],
            device_id=where_is(frm), device_id_type=MESH)

    own = pltpu.make_async_copy(reach_ref.at[me], moved.at[me], own_sem.at[0])
    own.start()

    @pl.loop(1, n)
    def _(k):
        send_reach(k).start()

    rows_f[...] = jnp.zeros_like(rows_f)
    rows_i[...] = jnp.zeros_like(rows_i)
    rows_f[0:2, 0:hands] = rank_ref[...].astype(jnp.float32)
    rows_i[0:2, 0:hands] = live_ref[...]
    dead = 1 - rows_i[0:2, :]
    low, high = bits_ref[0:1, :], bits_ref[1:2, :]
    ours = low + (1 << 26) + dead * (1 << 27)
    theirs = low + (1 << 27) + dead * (1 << 26)
    rows_i[0:2, :] = ours
    rows_i[2:3, :] = high
    rows_i[3:5, :] = theirs
    for tile in range(tiles):
        cut = slice(tile * LANE, (tile + 1) * LANE)
        cols_f[cut, :] = jnp.transpose(rows_f[:, cut])
        cols_i[cut, :] = jnp.transpose(rows_i[:, cut])

    @pl.loop(0, width // 16)
    def _(step):
        at = pl.ds(pl.multiple_of(step * 16, 16), 16)
        ranks, words = cols_f[at, :], cols_i[at, :]
        for board in range(2):
            shared = (rows_i[board:board + 1, :] & words[:, 3 + board:4 + board]) | (rows_i[2:3, :] & words[:, 2:3])
            sign = jnp.clip(rows_f[board:board + 1, :] - ranks[:, board:board + 1], -1.0, 1.0)
            pay[board, at, :] = jnp.where(shared == 0, sign, 0.0).astype(jnp.bfloat16)

    seq_parent = seq_parent_ref[...]

    @pl.loop(0, sets)
    def _(p):
        start = jnp.sum((seq_parent < p).astype(jnp.int32))
        last = jnp.sum((seq_parent <= p).astype(jnp.int32)) - 1
        for kid in range(KIDS):
            index = jnp.minimum(start + kid, last)
            kids_ref[p * KIDS + kid] = (index // 4) * 8 + lax.rem(index, 4)

    seqs = seq_parent.shape[1]

    @pl.loop(0, n)
    def _(src):
        row = lax.broadcasted_iota(jnp.int32, (8, 1), 0)
        seq = src * 4 + row % 4
        lane = lax.broadcasted_iota(jnp.int32, (8, seqs), 1)
        stake = jnp.sum(jnp.where(lane == seq, stake_ref[...], 0.0), axis=1, keepdims=True)
        limit = jnp.where(row < 4, board_seqs_ref[0], board_seqs_ref[1])
        scale_ref[pl.ds(pl.multiple_of(src * 8, 8), 8), :] = jnp.where(seq < limit, stake, 0.0)

    half = LANE // 2
    low_half = lax.broadcasted_iota(jnp.int32, (1, LANE), 1) < half

    @pl.loop(0, n)
    def _(src):
        turn_rows[pl.ds(src, 1), :] = jnp.where(low_half, turn_ref[2 * src], turn_ref[2 * src + 1])

    dense[...] = jnp.zeros_like(dense)
    set_row = lax.broadcasted_iota(jnp.int32, (sets, sets), 0)
    set_lane = lax.broadcasted_iota(jnp.int32, (sets, sets), 1)
    parent_col[...] = jnp.sum(jnp.where(set_row == set_lane, set_parent_ref[...], 0), axis=1, keepdims=True)

    own.wait()

    @pl.loop(1, n)
    def _(k):
        got_reach(k).wait_recv()

    chunk = 32
    first = lax.broadcasted_iota(jnp.int32, (chunk * 8, 1), 0) % 8 < 4

    @pl.loop(0, n // chunk)
    def _(part):
        src = pl.ds(part * chunk, chunk)
        dense[:, 0:hands] = moved[src].astype(jnp.float32).reshape(chunk * 8, hands).astype(jnp.bfloat16)
        rows = dense[...]
        at = pl.ds(pl.multiple_of(part * chunk * 8, chunk * 8), chunk * 8)
        scale = scale_ref[at, :]
        for nt in range(leaf.shape[1] // 256):
            cut = slice(nt * 256, (nt + 1) * 256)
            one = jnp.dot(rows, pay[0, :, cut], preferred_element_type=jnp.float32)
            two = jnp.dot(rows, pay[1, :, cut], preferred_element_type=jnp.float32)
            leaf[at, cut] = jnp.where(first, one, two) * scale

    @pl.loop(0, sets)
    def _(p):
        for board in range(2):
            row = leaf[pl.ds(kids_ref[p * KIDS] + 4 * board, 1), 0:width]
            for kid in range(1, KIDS):
                row = jnp.maximum(row, leaf[pl.ds(kids_ref[p * KIDS + kid] + 4 * board, 1), 0:width])
            river[board, pl.ds(p, 1), :] = row
            river_out[p, board:board + 1, :] = row[:, 0:hands]

    pieces = -(-hands // half)
    lines = D // 2
    for tile in range(tiles):
        one, two = (river[board, :, tile * LANE:(tile + 1) * LANE] for board in range(2))
        packed[2 * tile] = jnp.where(low_half, one, pltpu.roll(two, half, 1))
        packed[2 * tile + 1] = jnp.where(low_half, pltpu.roll(one, half, 1), two)

    def piece_of(grp, dev):
        return lax.rem(dev + D - 1, D) * G + grp

    mine = piece_of(g, d)

    def owner(piece):
        return (lax.rem(piece, G), lax.rem(piece // G + 1, D))

    def send_river(piece):
        return pltpu.make_async_remote_copy(
            src_ref=packed.at[piece], dst_ref=gathered.at[me], send_sem=send_c.at[piece], recv_sem=recv_c.at[me],
            device_id=owner(piece), device_id_type=MESH)

    @pl.loop(0, pieces)
    def _(piece):
        @pl.when(piece != mine)
        def _():
            send_river(piece).start()

    def send_turn(piece, slot, to):
        return pltpu.make_async_remote_copy(
            src_ref=best.at[piece], dst_ref=best.at[piece], send_sem=send_e.at[piece, slot], recv_sem=recv_e.at[piece],
            device_id=to, device_id_type=MESH)

    @pl.when(mine < pieces)
    def _():
        keep = pltpu.make_async_copy(packed.at[mine], gathered.at[me], own_sem.at[1])
        keep.start()
        keep.wait()

        @pl.loop(1, n)
        def _(k):
            frm = partner(k)
            pltpu.make_async_remote_copy(
                src_ref=packed.at[0], dst_ref=gathered.at[frm], send_sem=send_c.at[0], recv_sem=recv_c.at[frm],
                device_id=where_is(frm), device_id_type=MESH).wait_recv()

        group = 8
        psub = 32
        for turn0 in range(0, TURNS, group):
            for p0 in range(0, sets, psub):
                def add(src, accs):
                    block = gathered[src, p0:p0 + psub, :]
                    turn = jnp.broadcast_to(turn_rows[pl.ds(src, 1), :], (psub, LANE))
                    return tuple(acc + jnp.where(turn == turn0 + i, block, 0.0) for i, acc in enumerate(accs))
                accs = lax.fori_loop(
                    0, n, add, tuple(jnp.zeros((psub, LANE), jnp.float32) for _ in range(group)), unroll=4)
                for i in range(group):
                    chance[turn0 + i, p0:p0 + psub, :] = accs[i] + pltpu.roll(accs[i], half, 1)

        parents = jnp.broadcast_to(parent_col[...], (sets, LANE))

        @pl.loop(0, turn_sets)
        def _(q):
            chosen = parents == q
            rows = [jnp.max(jnp.where(chosen, chance[t], -jnp.inf), axis=0, keepdims=True) for t in range(TURNS)]
            early, late = jnp.concatenate(rows[:8], axis=0), jnp.concatenate(rows[8:], axis=0)
            best[mine, q] = jnp.where(low_half, early, late)

    line, core_of = d // 2, core

    def line_dev(k):
        return 2 * lax.rem(line + k, lines) + core_of

    def across(piece, run):
        for k in range(1, G):
            run(send_turn(piece, lines - 1 + k, (lax.rem(g + k, G), d)))

    def pair(piece, run):
        run(send_turn(piece, lines - 1 + G, (g, d + 1 - 2 * core)))

    def start(copy):
        copy.start()

    def finish(copy):
        copy.wait_send()

    def got(piece):
        send_turn(piece, 0, (lax.rem(g + 1, G), d)).wait_recv()

    @pl.when(mine < pieces)
    def _():
        for k in range(1, lines):
            start(send_turn(mine, k, (g, line_dev(k))))
        across(mine, start)
        pair(mine, start)

    @pl.loop(1, lines)
    def _(k):
        piece = piece_of(g, line_dev(k))

        @pl.when(piece < pieces)
        def _():
            got(piece)
            across(piece, start)
            pair(piece, start)

    @pl.loop(0, lines)
    def _(k):
        for j in range(1, G):
            piece = piece_of(lax.rem(g + j, G), line_dev(k))

            @pl.when(piece < pieces)
            def _():
                got(piece)
                pair(piece, start)

    @pl.loop(0, lines)
    def _(k):
        for j in range(G):
            piece = piece_of(lax.rem(g + j, G), line_dev(k) + 1 - 2 * core)

            @pl.when(piece < pieces)
            def _():
                got(piece)

    for tile in range(tiles):
        span = min(LANE, hands - tile * LANE)
        cut = slice(tile * LANE, tile * LANE + span)
        left = best[2 * tile]
        flipped = pltpu.roll(left, half, 2)
        if 2 * tile + 1 < pieces:
            right = best[2 * tile + 1]
            turn_out[:, 0:8, cut] = jnp.where(low_half, left, pltpu.roll(right, half, 2))[:, :, 0:span]
            turn_out[:, 8:16, cut] = jnp.where(low_half, flipped, right)[:, :, 0:span]
        else:
            turn_out[:, 0:8, cut] = left[:, :, 0:span]
            turn_out[:, 8:16, cut] = flipped[:, :, 0:span]

    @pl.when(mine < pieces)
    def _():
        for k in range(1, lines):
            finish(send_turn(mine, k, (g, line_dev(k))))

    @pl.loop(0, lines)
    def _(k):
        piece = piece_of(g, line_dev(k))

        @pl.when(piece < pieces)
        def _():
            across(piece, finish)

        for j in range(G):
            far = piece_of(lax.rem(g + j, G), line_dev(k))

            @pl.when(far < pieces)
            def _():
                pair(far, finish)

    @pl.loop(0, pieces)
    def _(piece):
        @pl.when(piece != mine)
        def _():
            send_river(piece).wait_send()

    @pl.loop(1, n)
    def _(k):
        send_reach(k).wait_send()


def local(G, D, reach, stake, hand_rank, hand_live, board_seqs, board_turn, seq_parent, set_parent):
    n = G * D
    own_seqs, boards, hands = reach.shape
    seqs = stake.shape[0]
    sets = set_parent.shape[0]
    tiles = -(-hands // LANE)
    width = tiles * LANE
    wide = -(-width // 256) * 256
    staged = jnp.transpose(reach.reshape(own_seqs, n, 2, hands), (1, 2, 0, 3)).reshape(n, 2 * own_seqs, hands)
    turn_sets = sets // 4
    vmem = pl.BlockSpec(memory_space=pltpu.VMEM)
    smem = pl.BlockSpec(memory_space=pltpu.SMEM)
    river, best = pl.pallas_call(
        functools.partial(kernel, G, D, hands),
        out_shape=(
            jax.ShapeDtypeStruct((sets, 2, hands), jnp.float32),
            jax.ShapeDtypeStruct((turn_sets, TURNS, hands), jnp.float32),
        ),
        in_specs=[smem, smem, vmem, vmem, vmem, vmem, vmem, vmem, vmem],
        out_specs=(vmem, vmem),
        scratch_shapes=[
            pltpu.SMEM((sets * KIDS,), jnp.int32),
            pltpu.VMEM((n * 8, 1), jnp.float32),
            pltpu.VMEM((sets, 1), jnp.int32),
            pltpu.VMEM((n, LANE), jnp.int32),
            pltpu.VMEM((n, 8, hands), jnp.bfloat16),
            pltpu.VMEM((256, width), jnp.bfloat16),
            pltpu.VMEM((8, wide), jnp.float32),
            pltpu.VMEM((8, wide), jnp.int32),
            pltpu.VMEM((width, 8), jnp.float32),
            pltpu.VMEM((width, 8), jnp.int32),
            pltpu.VMEM((2, width, wide), jnp.bfloat16),
            pltpu.VMEM((n * 8, wide), jnp.float32),
            pltpu.VMEM((2, sets, width), jnp.float32),
            pltpu.VMEM((2 * tiles, sets, LANE), jnp.float32),
            pltpu.VMEM((n, sets, LANE), jnp.float32),
            pltpu.VMEM((TURNS, sets, LANE), jnp.float32),
            pltpu.VMEM((2 * tiles, turn_sets, 8, LANE), jnp.float32),
            pltpu.SemaphoreType.DMA((n,)),
            pltpu.SemaphoreType.DMA((n,)),
            pltpu.SemaphoreType.DMA((2 * tiles,)),
            pltpu.SemaphoreType.DMA((n,)),
            pltpu.SemaphoreType.DMA((2 * tiles, D // 2 + G)),
            pltpu.SemaphoreType.DMA((2 * tiles,)),
            pltpu.SemaphoreType.DMA((2,)),
        ],
        compiler_params=pltpu.CompilerParams(
            collective_id=0, has_side_effects=True, vmem_limit_bytes=56 << 20),
    )(board_turn[:, 0], board_seqs, seq_parent[None, :], set_parent[None, :], stake[None, :], staged,
      hand_rank, hand_live, jnp.asarray(card_bits(hands, wide)))
    return river, best


def solution(mesh):
    axes = ("grp", "dev")
    in_specs = (
        P(axes, None, None),
        P(),
        P(axes, None),
        P(axes, None),
        P(axes),
        P(),
        P(),
        P(),
    )
    out_specs = (P(None, axes, None), P())
    body = functools.partial(local, mesh.shape["grp"], mesh.shape["dev"])
    return jax.shard_map(body, mesh=mesh, in_specs=in_specs, out_specs=out_specs, check_vma=False)
```

time: 67.4 us -> 64.4 us (0.955)
  the two profiles are of different devices: /device:TPU:27 before, /device:TPU:1 now
where the time goes in v2:
time: 64.4 us; the launch traced here: 64.2 us
  Pallas kernels  58 us (90%)
  local copies, waits for them, and re-layouts  5.57 us (9%)
  between operations  0.65 us (1%)
    pallas_call x1, Pallas kernels, local(): pl.pallas_call(functools.partial(kernel, G, D, hands), out_shape=(jax.Sha...  58 us
    unnamed x4, local copies, waits for them, and re-layouts  2.69 us
    reshape x1, local copies, waits for them, and re-layouts, local(): reach.reshape(own_seqs, n, 2, hands)  1.67 us

profile of v2, /device:TPU:1, one launch (start us, length us, event | category | flops | bytes accessed | tf_op | source)
XLA Modules:
  0.0 64.2 jit_solution(4087211694145011268)
XLA Ops:
  0.6 1.7 %copy.12 = bf16[4,64,1326]{2,0,1:T(4,128)(2,1)S(1)} copy(bf16[4,64,1326]{2,1,0:T(8,128)(2,1)} %param.9) | data formatting | bytes 1357824 | tf_op jit(solution)/shard_map/reshape | solution.py:346
  2.3 1.2 %reshape.11.reach_ref = bf16[32,8,1326]{2,1,0:T(8,128)(2,1)} reshape(bf16[32,2,4,1326]{3,2,1,0:T(4,128)(2,1)S(1)} %bitcast.7) | data formatting | bytes 1357824 | tf_op jit(solution)/shard_map/reshape | solution.py:346
  3.5 58.0 %shard_map.104 = (f32[32,2,1326]{2,1,0:T(2,128)}, f32[8,16,1326]{2,1,0:T(8,128)}) custom-call(s32[64]{0:T(128)} %bitcast.8, s32[2]{0:T(128)} %board_seqs_ref.1, s32[1,128]{1,0:T(1,128)} %bitcast.9, s32[1,32]{1,0:T(1,128)} %bitcast.10, f32[1,128]{1,0:T(1,128)} %bitcast.11, bf16[32,8,1326]{2,1,0:T(8,128)(2,1)} %reshape.11.reach_ref, s32[2,1326]{1,0:T(2,128)} %rank_ref.1, ...), custom_call_target="tpu_custom_call" | custom-call | tf_op jit(solution)/shard_map/pallas_call | solution.py:350
  61.5 0.0 copy-start
  61.5 1.8 %copy.15 = f32[32,2,1326]{2,1,0:T(2,128)} copy(f32[32,2,1326]{2,1,0:T(2,128)} %get-tuple-element.4) | data formatting | bytes 678912
  63.3 0.0 copy-done
  63.3 0.9 %copy.16 = f32[8,16,1326]{2,1,0:T(8,128)} copy(f32[8,16,1326]{2,1,0:T(8,128)S(1)} %copy-done) | data formatting | bytes 1357824
Async XLA Ops:
  61.5 1.8 %copy-start = (f32[8,16,1326]{2,1,0:T(8,128)S(1)}, f32[8,16,1326]{2,1,0:T(8,128)}, u32[]{:S(2)}) copy-start(f32[8,16,1326]{2,1,0:T(8,128)} %get-tuple-element.5) | copy-start | bytes 2036740

commit v3 on v2

--- a/solution.py
+++ b/solution.py
@@ -106,24 +106,24 @@
 
     seq_parent = seq_parent_ref[...]
 
-    @pl.loop(0, sets)
-    def _(p):
-        start = jnp.sum((seq_parent < p).astype(jnp.int32))
-        last = jnp.sum((seq_parent <= p).astype(jnp.int32)) - 1
-        for kid in range(KIDS):
-            index = jnp.minimum(start + kid, last)
-            kids_ref[p * KIDS + kid] = (index // 4) * 8 + lax.rem(index, 4)
+    block = 16
+
+    @pl.loop(0, sets // block)
+    def _(step):
+        p0 = step * block
+        starts = [jnp.sum((seq_parent < p0 + i).astype(jnp.int32)) for i in range(block + 1)]
+        for i in range(block):
+            for kid in range(KIDS):
+                index = jnp.minimum(starts[i] + kid, starts[i + 1] - 1)
+                kids_ref[(p0 + i) * KIDS + kid] = index + (index // 4) * 4
 
     seqs = seq_parent.shape[1]
-
-    @pl.loop(0, n)
-    def _(src):
-        row = lax.broadcasted_iota(jnp.int32, (8, 1), 0)
-        seq = src * 4 + row % 4
-        lane = lax.broadcasted_iota(jnp.int32, (8, seqs), 1)
-        stake = jnp.sum(jnp.where(lane == seq, stake_ref[...], 0.0), axis=1, keepdims=True)
-        limit = jnp.where(row < 4, board_seqs_ref[0], board_seqs_ref[1])
-        scale_ref[pl.ds(pl.multiple_of(src * 8, 8), 8), :] = jnp.where(seq < limit, stake, 0.0)
+    row = lax.broadcasted_iota(jnp.int32, (n * 8, 1), 0)
+    seq = (row >> 3) * 4 + (row & 3)
+    lane = lax.broadcasted_iota(jnp.int32, (n * 8, seqs), 1)
+    stake = jnp.sum(jnp.where(lane == seq, stake_ref[...], 0.0), axis=1, keepdims=True)
+    limit = jnp.where((row & 4) == 0, board_seqs_ref[0], board_seqs_ref[1])
+    scale_ref[...] = jnp.where(seq < limit, stake, 0.0)
 
     half = LANE // 2
     low_half = lax.broadcasted_iota(jnp.int32, (1, LANE), 1) < half

time: 64.4 us -> 61.5 us (0.955)
  Pallas kernels: 58 us -> 55 us
    pallas_call x1, Pallas kernels: 58 us -> 55 us  [local(): pl.pallas_call(functools.partial(kernel, G, D, hands), out_shape=(jax.Sha...]
where the time goes in v3:
time: 61.5 us; the launch traced here: 61.3 us
  Pallas kernels  55 us (89%)
  local copies, waits for them, and re-layouts  5.57 us (9%)
  between operations  0.65 us (1%)
    pallas_call x1, Pallas kernels, local(): pl.pallas_call(functools.partial(kernel, G, D, hands), out_shape=(jax.Sha...  55 us
    unnamed x4, local copies, waits for them, and re-layouts  2.69 us
    reshape x1, local copies, waits for them, and re-layouts, local(): reach.reshape(own_seqs, n, 2, hands)  1.67 us

profile of v3, /device:TPU:1, one launch (start us, length us, event | category | flops | bytes accessed | tf_op | source)
XLA Modules:
  0.0 61.3 jit_solution(10982978714518031049)
XLA Ops:
  0.6 1.7 %copy.12 = bf16[4,64,1326]{2,0,1:T(4,128)(2,1)S(1)} copy(bf16[4,64,1326]{2,1,0:T(8,128)(2,1)} %param.9) | data formatting | bytes 1357824 | tf_op jit(solution)/shard_map/reshape | solution.py:346
  2.3 1.2 %reshape.11.reach_ref = bf16[32,8,1326]{2,1,0:T(8,128)(2,1)} reshape(bf16[32,2,4,1326]{3,2,1,0:T(4,128)(2,1)S(1)} %bitcast.7) | data formatting | bytes 1357824 | tf_op jit(solution)/shard_map/reshape | solution.py:346
  3.5 55.0 %shard_map.104 = (f32[32,2,1326]{2,1,0:T(2,128)}, f32[8,16,1326]{2,1,0:T(8,128)}) custom-call(s32[64]{0:T(128)} %bitcast.8, s32[2]{0:T(128)} %board_seqs_ref.1, s32[1,128]{1,0:T(1,128)} %bitcast.9, s32[1,32]{1,0:T(1,128)} %bitcast.10, f32[1,128]{1,0:T(1,128)} %bitcast.11, bf16[32,8,1326]{2,1,0:T(8,128)(2,1)} %reshape.11.reach_ref, s32[2,1326]{1,0:T(2,128)} %rank_ref.1, ...), custom_call_target="tpu_custom_call" | custom-call | tf_op jit(solution)/shard_map/pallas_call | solution.py:350
  58.6 0.0 copy-start
  58.6 1.8 %copy.15 = f32[32,2,1326]{2,1,0:T(2,128)} copy(f32[32,2,1326]{2,1,0:T(2,128)} %get-tuple-element.4) | data formatting | bytes 678912
  60.4 0.0 copy-done
  60.4 0.9 %copy.16 = f32[8,16,1326]{2,1,0:T(8,128)} copy(f32[8,16,1326]{2,1,0:T(8,128)S(1)} %copy-done) | data formatting | bytes 1357824
Async XLA Ops:
  58.6 1.8 %copy-start = (f32[8,16,1326]{2,1,0:T(8,128)S(1)}, f32[8,16,1326]{2,1,0:T(8,128)}, u32[]{:S(2)}) copy-start(f32[8,16,1326]{2,1,0:T(8,128)} %get-tuple-element.5) | copy-start | bytes 2036740

commit v4 on v3

--- a/solution.py
+++ b/solution.py
@@ -269,8 +269,8 @@
         @pl.when(piece < pieces)
         def _():
             got(piece)
+            pair(piece, start)
             across(piece, start)
-            pair(piece, start)
 
     @pl.loop(0, lines)
     def _(k):
@@ -353,7 +353,7 @@
             jax.ShapeDtypeStruct((sets, 2, hands), jnp.float32),
             jax.ShapeDtypeStruct((turn_sets, TURNS, hands), jnp.float32),
         ),
-        in_specs=[smem, smem, vmem, vmem, vmem, vmem, vmem, vmem, vmem],
+        in_specs=[smem, smem, vmem, vmem, vmem, pl.BlockSpec(memory_space=pl.ANY), vmem, vmem, vmem],
         out_specs=(vmem, vmem),
         scratch_shapes=[
             pltpu.SMEM((sets * KIDS,), jnp.int32),

time: 61.5 us -> 61.3 us (level)
  no operation moved by 1% of the time
where the time goes in v4:
time: 61.3 us; the launch traced here: 61.1 us
  Pallas kernels  54.9 us (90%)
  local copies, waits for them, and re-layouts  5.57 us (9%)
  between operations  0.65 us (1%)
    pallas_call x1, Pallas kernels, local(): pl.pallas_call(functools.partial(kernel, G, D, hands), out_shape=(jax.Sha...  54.9 us
    unnamed x4, local copies, waits for them, and re-layouts  2.69 us
    reshape x1, local copies, waits for them, and re-layouts, local(): reach.reshape(own_seqs, n, 2, hands)  1.67 us

profile of v4, /device:TPU:1, one launch (start us, length us, event | category | flops | bytes accessed | tf_op | source)
XLA Modules:
  0.0 61.1 jit_solution(5866003231358378943)
XLA Ops:
  0.6 1.7 %copy.12 = bf16[4,64,1326]{2,0,1:T(4,128)(2,1)S(1)} copy(bf16[4,64,1326]{2,1,0:T(8,128)(2,1)} %param.9) | data formatting | bytes 1357824 | tf_op jit(solution)/shard_map/reshape | solution.py:346
  2.3 1.2 %reshape.11.reach_ref = bf16[32,8,1326]{2,1,0:T(8,128)(2,1)} reshape(bf16[32,2,4,1326]{3,2,1,0:T(4,128)(2,1)S(1)} %bitcast.7) | data formatting | bytes 1357824 | tf_op jit(solution)/shard_map/reshape | solution.py:346
  3.5 54.9 %shard_map.104 = (f32[32,2,1326]{2,1,0:T(2,128)}, f32[8,16,1326]{2,1,0:T(8,128)}) custom-call(s32[64]{0:T(128)} %bitcast.8, s32[2]{0:T(128)} %board_seqs_ref.1, s32[1,128]{1,0:T(1,128)} %bitcast.9, s32[1,32]{1,0:T(1,128)} %bitcast.10, f32[1,128]{1,0:T(1,128)} %bitcast.11, bf16[32,8,1326]{2,1,0:T(8,128)(2,1)} %reshape.11.reach_ref, s32[2,1326]{1,0:T(2,128)} %rank_ref.1, ...), custom_call_target="tpu_custom_call" | custom-call | tf_op jit(solution)/shard_map/pallas_call | solution.py:350
  58.4 0.0 copy-start
  58.4 1.8 %copy.15 = f32[32,2,1326]{2,1,0:T(2,128)} copy(f32[32,2,1326]{2,1,0:T(2,128)} %get-tuple-element.4) | data formatting | bytes 678912
  60.2 0.0 copy-done
  60.2 0.9 %copy.16 = f32[8,16,1326]{2,1,0:T(8,128)} copy(f32[8,16,1326]{2,1,0:T(8,128)S(1)} %copy-done) | data formatting | bytes 1357824
Async XLA Ops:
  58.4 1.8 %copy-start = (f32[8,16,1326]{2,1,0:T(8,128)S(1)}, f32[8,16,1326]{2,1,0:T(8,128)}, u32[]{:S(2)}) copy-start(f32[8,16,1326]{2,1,0:T(8,128)} %get-tuple-element.5) | copy-start | bytes 2036740
